TPU v7x, 32 devices: a whole 2x2x4 slice. The times are simulated.
32 devices in a mesh: seq: 8 (over z, y), lane: 4 (over x, core).
Axes of the slice: x: 2, y: 2, z: 4, core: 2. Of those that a mesh axis runs over, the one named last changes fastest.
Arguments:
- tokens_in: bfloat16 [3072, 8192], P('seq', 'lane'), may hold values from -6 to 6
- gate_weight: bfloat16 [8192, 1024], P(None, 'lane'), may hold values from -0.0625 to 0.0625
- up_weight: bfloat16 [8192, 1024], P(None, 'lane'), may hold values from -0.0625 to 0.0625
- output_grad: bfloat16 [3072, 4096], P('seq', 'lane'), may hold values from -0.15234375 to 0.15234375
- input_basis: float32 [1024, 1024], P('seq'), may hold values from -0.1875 to 0.1875
- output_basis: float32 [4, 1024, 1024], P('lane', 'seq'), may hold values from -0.1875 to 0.1875
- shard_order: int32 [8], replicated, may hold values from 0 to 7, each once
Outputs:
- eigenvalues: float32 [4, 1024, 1024], P('lane', 'seq')
All inputs are finite; a program needn't handle non-finite values.
Results may differ from a plain program's by a relative error of at most 0.0029.
Values may be sent and summed in bfloat16 or wider, within the bound.
A program may use at most 128 MiB of HBM per device.

v0:
```python
import jax
import jax.numpy as jnp
from jax import lax
from jax.sharding import PartitionSpec as P


def on_device(
    tokens_in, gate_weight, up_weight, output_grad, input_basis, output_basis, shard_order
):
    full_tokens, full_grads = (
        lax.all_gather(tokens_in, "lane", axis=1, tiled=True),
        lax.all_gather(output_grad, "lane", axis=1, tiled=True),
    )
    gate_proj = jnp.dot(full_tokens, gate_weight, preferred_element_type=jnp.float32)
    up_proj = jnp.dot(full_tokens, up_weight, preferred_element_type=jnp.float32)
    hidden = (jax.nn.silu(gate_proj) * up_proj).astype(jnp.bfloat16)
    lane_count = lax.axis_size("lane")
    shard_count = lax.axis_size("seq")
    columns = gate_weight.shape[1]
    tile = columns * lane_count
    position = lax.dynamic_index_in_dim(shard_order, lax.axis_index("seq"), 0, keepdims=False)
    member = 2 * position // shard_count
    first_mask = (member == 0).astype(jnp.float32)
    second_mask = 1.0 - first_mask
    partial_value = lax.dot_general(
        full_grads, hidden, (((0,), (0,)), ((), ())), preferred_element_type=jnp.float32
    )
    partial_value = partial_value.reshape(lane_count, tile, columns)
    moved = lax.all_to_all(partial_value, "lane", split_axis=0, concat_axis=2, tiled=True)
    stacked = jnp.concatenate([moved * first_mask, moved * second_mask], axis=1)
    slab = lax.psum_scatter(stacked, "seq", scatter_dimension=1, tiled=True)
    slab = slab[0]
    block = slab
    turned = lax.dot_general(
        lax.all_gather(input_basis, "seq", axis=0, tiled=True),
        block,
        (((0,), (1,)), ((), ())),
        precision=lax.Precision.HIGHEST,
        preferred_element_type=jnp.float32,
    )
    swapped = lax.all_to_all(turned, "seq", split_axis=0, concat_axis=1, tiled=True)
    shaped = swapped.reshape(swapped.shape[0], 2, tile)
    block = shaped
    rotated = jnp.einsum(
        "jsr,ri->jsi",
        block,
        lax.all_gather(output_basis[0], "seq", axis=0, tiled=True),
        precision=lax.Precision.HIGHEST,
    )
    estimate = jnp.mean(rotated * rotated, axis=1)
    return estimate[None]


def solution(mesh):
    return jax.shard_map(
        on_device,
        mesh=mesh,
        in_specs=(
            P("seq", "lane"),
            P(None, "lane"),
            P(None, "lane"),
            P("seq", "lane"),
            P("seq", None),
            P("lane", "seq", None),
            P(),
        ),
        out_specs=P("lane", "seq", None),
        check_vma=False,
    )
```

profile of v0, /device:TPU:13, one launch (start us, length us, event | category | flops | bytes accessed | tf_op | source)
XLA Modules:
  0.0 415.3 jit_solution(13351423205895539606)
XLA Ops:
  6.5 0.0 all-gather.6.cloned.1.call-start
  6.5 0.7 all-gather.6.cloned.1.call-update
  7.3 0.0 all-gather.8.cloned.1.call-start
  7.3 0.7 all-gather.8.cloned.1.call-update
  8.0 0.0 all-gather.10.cloned.1.call-start
  8.1 0.7 all-gather.10.cloned.1.call-update
  8.7 48.1 %all-gather.6.cloned.1.call-done = bf16[384,8192]{1,0:T(8,128)(2,1)} async-done(((bf16[384,2048]{1,0:T(8,128)(2,1)}), bf16[384,8192]{1,0:T(8,128)(2,1)}) %all-gather.6.cloned.1.call-update) | async-done | bytes 6291472 | tf_op jit(solution)/shard_map/all_gather | solution.py:11
  56.8 5.8 %fusion.18 = f32[384,256]{1,0:T(8,128)S(1)} fusion(bf16[384,8192]{1,0:T(8,128)(2,1)} %all-gather.6.cloned.1.call-done, bf16[8192,256]{1,0:T(8,128)(2,1)} %param.8), kind=kOutput, calls=%fused_computation.22 | convolution fusion | flops 1610612736 | bytes 10878976 | tf_op jit(solution)/shard_map/dot_general | solution.py:14
  62.6 24.3 %all-gather.8.cloned.1.call-done = bf16[384,4096]{1,0:T(8,128)(2,1)} async-done(((bf16[384,1024]{1,0:T(8,128)(2,1)}), bf16[384,4096]{1,0:T(8,128)(2,1)}) %all-gather.8.cloned.1.call-update) | async-done | bytes 3145744 | tf_op jit(solution)/shard_map/all_gather | solution.py:12
  86.9 12.2 %fusion.9 = f32[256,4096]{1,0:T(8,128)} fusion(bf16[384,4096]{1,0:T(8,128)(2,1)} %all-gather.8.cloned.1.call-done, bf16[384,8192]{1,0:T(8,128)(2,1)} %all-gather.6.cloned.1.call-done, bf16[8192,256]{1,0:T(8,128)(2,1)} %param.9, f32[384,256]{1,0:T(8,128)S(1)} %fusion.18), kind=kOutput, calls=%fused_computation.11 | convolution fusion | flops 2416508928 | bytes 18219008 | tf_op jit(solution)/shard_map/dot_general | solution.py:25
  99.0 4.7 %copy.16 = f32[32,4,8,1024]{3,2,0,1:T(8,128)} copy(f32[32,4,8,1024]{3,2,1,0:T(8,128)} %bitcast.45) | data formatting | bytes 8388608 | tf_op jit(solution)/shard_map/reshape | solution.py:28
  103.8 0.0 copy-start
  103.8 5.3 %all-to-all-start = ((f32[4,1024,256]{1,2,0:T(8,128)}), f32[4,1024,256]{1,2,0:T(8,128)}, u32[]{:S(2)}, u32[]{:S(2)}) async-start(f32[4,1024,256]{1,2,0:T(8,128)} %bitcast.46), calls=%async_computation | async-start | bytes 8388608 | tf_op jit(solution)/shard_map/all_to_all | solution.py:29
  109.1 0.0 reduce-scatter.2.cloned.1.call-start
  109.1 0.0 copy-done
  109.1 0.6 dynamic_slice.4
  110.3 46.0 %all-to-all-done = f32[4,1024,256]{1,2,0:T(8,128)} async-done(((f32[4,1024,256]{1,2,0:T(8,128)}), f32[4,1024,256]{1,2,0:T(8,128)}, u32[]{:S(2)}, u32[]{:S(2)}) %all-to-all-start) | async-done | bytes 4194336 | tf_op jit(solution)/shard_map/all_to_all | solution.py:29
  156.4 3.2 broadcast_multiply_fusion.1
  159.6 3.9 pad_maximum_fusion
  163.5 0.0 reduce-scatter.2.cloned.1.call-update
  163.5 0.0 all-gather.12.cloned.1.call-start
  163.6 0.5 all-gather.12.cloned.1.call-update
  164.1 0.0 all-gather.10.cloned.1.call-done
  164.1 146.3 %reduce-scatter.2.cloned.1.call-done = f32[1,256,1024]{1,2,0:T(8,128)} async-done(((f32[1,2048,1024]{1,2,0:T(8,128)}), f32[1,256,1024]{1,2,0:T(8,128)}) %reduce-scatter.2.cloned.1.call-update) | async-done | bytes 1048592 | tf_op jit(solution)/shard_map/reduce_scatter | solution.py:31
  310.4 5.9 %convolution_bitcast_fusion = f32[32,8,8,128]{3,2,1,0:T(8,128)S(1)} fusion(f32[1024,1024]{1,0:T(8,128)} %all-gather.10.cloned.1.call-done, f32[1,256,1024]{1,2,0:T(8,128)} %reduce-scatter.2.cloned.1.call-done), kind=kOutput, calls=%fused_computation.7 | convolution fusion | flops 3221225472 | bytes 6291456 | tf_op jit(solution)/shard_map/dot_general | solution.py:34
  316.3 1.0 copy.17
  317.3 5.2 %all-to-all-start.1 = ((f32[8,128,256]{1,2,0:T(8,128)}), f32[8,128,256]{1,2,0:T(8,128)S(1)}, u32[]{:S(2)}, u32[]{:S(2)}) async-start(f32[8,128,256]{1,2,0:T(8,128)} %bitcast.44), calls=%async_computation.2 | async-start | bytes 2097152 | tf_op jit(solution)/shard_map/all_to_all | solution.py:41
  322.6 79.5 %all-gather.12.cloned.1.call-done = f32[1,1024,1024]{2,1,0:T(8,128)} async-done(((f32[1,128,1024]{2,1,0:T(8,128)}), f32[1,1024,1024]{2,1,0:T(8,128)}) %all-gather.12.cloned.1.call-update) | async-done | bytes 4194320 | tf_op jit(solution)/shard_map/all_gather | solution.py:47
  402.1 0.0 all-to-all-done.1
  402.1 5.8 %fusion.5 = f32[128,1024]{1,0:T(8,128)S(1)} fusion(f32[128,2,1024]{0,2,1:T(8,128)S(1)} %bitcast.49, f32[1,1024,1024]{2,1,0:T(8,128)} %all-gather.12.cloned.1.call-done), kind=kOutput, calls=%fused_computation.8 | convolution fusion | flops 3221618688 | bytes 5767168 | tf_op jit(solution)/shard_map/jsr,ri->jsi/dot_general | solution.py:44
  407.9 0.8 multiply_bitcast_fusion
Async XLA Ops:
  6.5 50.3 %all-gather.6.cloned.1.call-start = ((), (), s32[]{:S(2)}) async-start(), calls=%async_computation.3 | async-start | bytes 7864320 | tf_op jit(solution)/shard_map/all_gather | solution.py:11
  7.3 79.6 %all-gather.8.cloned.1.call-start = ((), (), s32[]{:S(2)}) async-start(), calls=%async_computation.4 | async-start | bytes 3932160 | tf_op jit(solution)/shard_map/all_gather | solution.py:12
  8.0 156.1 %all-gather.10.cloned.1.call-start = ((), (), s32[]{:S(2)}) async-start(), calls=%async_computation.6 | async-start | bytes 4718592 | tf_op jit(solution)/shard_map/all_gather | solution.py:35
  103.8 5.3 %copy-start = (s32[8]{0:T(128)S(1)}, s32[8]{0:T(128)}, u32[]{:S(2)}) copy-start(s32[8]{0:T(128)} %param.13) | copy-start | bytes 100
  103.8 52.6 %all-to-all-start = ((f32[4,1024,256]{1,2,0:T(8,128)}), f32[4,1024,256]{1,2,0:T(8,128)}, u32[]{:S(2)}, u32[]{:S(2)}) async-start(f32[4,1024,256]{1,2,0:T(8,128)} %bitcast.46), calls=%async_computation | async-start | bytes 8388608 | tf_op jit(solution)/shard_map/all_to_all | solution.py:29
  109.1 201.3 %reduce-scatter.2.cloned.1.call-start = ((), (), s32[]{:S(2)}) async-start(), calls=%async_computation.5 | async-start | bytes 9437184 | tf_op jit(solution)/shard_map/reduce_scatter | solution.py:31
  163.5 238.5 %all-gather.12.cloned.1.call-start = ((), (), s32[]{:S(2)}) async-start(), calls=%async_computation.7 | async-start | bytes 4718592 | tf_op jit(solution)/shard_map/all_gather | solution.py:47
  317.3 84.7 %all-to-all-start.1 = ((f32[8,128,256]{1,2,0:T(8,128)}), f32[8,128,256]{1,2,0:T(8,128)S(1)}, u32[]{:S(2)}, u32[]{:S(2)}) async-start(f32[8,128,256]{1,2,0:T(8,128)} %bitcast.44), calls=%async_computation.2 | async-start | bytes 2097152 | tf_op jit(solution)/shard_map/all_to_all | solution.py:41
Sparse Core Ops, SparseCore 0:
  8.9 47.8 all-gather.5
  58.4 28.4 all-gather.7
  89.0 69.4 all-gather.9
  163.6 146.7 reduce-scatter.1
  312.4 89.6 all-gather.11
where the time goes:
time: 420 us; the launch traced here: 415 us
  waiting for transfers between devices  347 us (83%)
  matrix products  29.7 us (7%)
  between operations  13.9 us (3%)
  starting transfers between devices  10.6 us (3%)
  other arithmetic  7.96 us (2%)
  local copies, waits for them, and re-layouts  6.37 us (2%)
    reduce_scatter x1, waiting for transfers between devices, on_device(): slab = lax.psum_scatter(stacked, 'seq', scatter_dimension=1, tiled=True)  146 us
    all_gather x1, waiting for transfers between devices, on_device(): lax.all_gather(output_basis[0], 'seq', axis=0, tiled=True)  79.5 us
    all_gather x1, waiting for transfers between devices, on_device(): lax.all_gather(tokens_in, 'lane', axis=1, tiled=True)  48.1 us
    all_to_all x1, waiting for transfers between devices, on_device(): lax.all_to_all(partial_value, 'lane', split_axis=0, concat_axis=2, tiled=...  46 us
    all_gather x1, waiting for transfers between devices, on_device(): lax.all_gather(output_grad, 'lane', axis=1, tiled=True)  24.3 us
    dot_general x1, matrix products, on_device(): lax.dot_general(full_grads, hidden, (((0,), (0,)), ((), ())), preferred_e...  12.2 us
  transfers between devices with their start and end apart: 7, of which 5 were waited for; matrix products, arithmetic and copies ran while one was open for 9% of the time, Pallas kernels for 0%

commit v1 on v0

v1 whole, which is shorter than its diff:
```python
import functools

import jax
import jax.numpy as jnp
from jax import lax
from jax.experimental import pallas as pl
from jax.experimental.pallas import tpu as pltpu
from jax.sharding import PartitionSpec as P

F32 = jnp.float32
BF16 = jnp.bfloat16
CHUNKS = 4


def split(value):
    high = value.astype(BF16)
    return high, (value - high.astype(F32)).astype(BF16)


def dot(a, b):
    return jnp.dot(a, b, preferred_element_type=F32)


def dot_first(a, b):
    return lax.dot_general(a, b, (((0,), (0,)), ((), ())), preferred_element_type=F32)


def kernel(
    n, order, tok_in, gate_in, up_in, grad_in, ib_in, ob_in, out,
    gate_w, up_w, tok, grad, ib, ob, acc_g, acc_u, hid,
    a_hi, a_lo, b_hi, b_lo, r_send, r_recv, sum0, sum1,
    load_sem, own_sem, x_send, x_recv, c_send, c_recv, f_send, f_recv,
    h_send, h_recv, ob_send, ob_recv, ib_send, ib_recv, e_send, e_recv,
    r_ssem, r_rsem,
):
    s, l = lax.axis_index("seq"), lax.axis_index("lane")
    px, pc = l // 2, l % 2
    part, across, diag = 2 * px + 1 - pc, 2 * (1 - px) + pc, 2 * (1 - px) + 1 - pc
    half = n // 2
    y, z = s % 2, s // 2
    ring = z + y * (n - 1 - 2 * z)

    def seq_of(r):
        r = lax.rem(r + 2 * n, n)
        b = r // half
        return (1 - b) * 2 * r + b * (2 * (n - 1 - r) + 1)

    nxt, prv = seq_of(ring + 1), seq_of(ring - 1)

    def remote(src, dst, ssem, rsem, seq, lane):
        return pltpu.make_async_remote_copy(
            src_ref=src, dst_ref=dst, send_sem=ssem, recv_sem=rsem,
            device_id=(seq, lane), device_id_type=pl.DeviceIdType.MESH,
        )

    loads = [
        pltpu.make_async_copy(gate_in, gate_w, load_sem.at[0]),
        pltpu.make_async_copy(up_in, up_w, load_sem.at[1]),
        pltpu.make_async_copy(grad_in, grad, load_sem.at[2]),
        pltpu.make_async_copy(ib_in, ib.at[s], load_sem.at[3]),
        pltpu.make_async_copy(ob_in, ob.at[s], load_sem.at[4]),
    ]
    depth = tok_in.shape[1]
    width = depth // CHUNKS
    own = [
        pltpu.make_async_copy(
            tok_in.at[:, pl.ds(i * width, width)], tok.at[0, i], own_sem.at[i]
        )
        for i in range(CHUNKS)
    ]
    for copy in loads + own:
        copy.start()

    barrier = pltpu.get_barrier_semaphore()
    for d in range(1, n):
        pl.semaphore_signal(
            barrier, inc=1, device_id=(lax.rem(s + d, n), l),
            device_id_type=pl.DeviceIdType.MESH,
        )
    for lane in (part, across):
        pl.semaphore_signal(
            barrier, inc=1, device_id=(s, lane), device_id_type=pl.DeviceIdType.MESH
        )
    pl.semaphore_wait(barrier, n + 1)

    to_across, to_part, passed = [], [], []
    for i in range(CHUNKS):
        piece = tok_in.at[:, pl.ds(i * width, width)]
        to_across.append(remote(piece, tok.at[2, i], x_send.at[i], x_recv.at[i], s, across))
        to_part.append(remote(piece, tok.at[1, i], c_send.at[i], c_recv.at[i], s, part))
        passed.append(remote(tok.at[2, i], tok.at[3, i], f_send.at[i], f_recv.at[i], s, part))
    for copy in to_across:
        copy.start()

    tile = ob.shape[2]
    wide = tile // 2
    narrow = tile // 4
    ib_base = pc * wide

    def ring_copies(t):
        made = []
        for way in range(2):
            owner = seq_of(ring - t) if way == 0 else seq_of(ring + t)
            target = nxt if way == 0 else prv
            columns = pl.ds(way * wide, wide)
            small = pl.ds(pl.multiple_of(ib_base + way * narrow, narrow), narrow)
            ob_src = ob_in.at[:, columns] if t == 0 else ob.at[owner, :, columns]
            ib_src = ib_in.at[:, small] if t == 0 else ib.at[owner, :, small]
            made.append(remote(
                ob_src, ob.at[owner, :, columns],
                ob_send.at[way, t], ob_recv.at[way, t], target, l))
            made.append(remote(
                ib_src, ib.at[owner, :, small],
                ib_send.at[way, t], ib_recv.at[way, t], target, l))
        return made

    steps = [ring_copies(t) for t in range(n - 1)]
    swaps = []

    def ring_arrive(t):
        for copy in steps[t]:
            copy.wait_recv()
        if t + 1 < n - 1:
            for copy in steps[t + 1]:
                copy.start()
        for way in range(2):
            owner = seq_of(ring - t - 1) if way == 0 else seq_of(ring + t + 1)
            small = pl.ds(pl.multiple_of(ib_base + way * narrow, narrow), narrow)
            piece = ib.at[owner, :, small]
            swap = remote(piece, piece, e_send.at[way, t], e_recv.at[way, t], s, part)
            swap.start()
            swaps.append(swap)

    for copy in steps[0]:
        copy.start()
    for copy in to_part:
        copy.start()

    loads[0].wait()
    loads[1].wait()

    def multiply(slot, i, lane, first=False):
        rows = pl.ds(pl.multiple_of(lane * depth + i * width, width), width)
        piece = tok[slot, i]
        g = dot(piece, gate_w[rows, :])
        u = dot(piece, up_w[rows, :])
        if first:
            acc_g[...] = g
            acc_u[...] = u
        else:
            acc_g[...] += g
            acc_u[...] += u

    def arrive(i):
        to_across[i].wait_recv()
        passed[i].start()
        multiply(2, i, across)
        passed[i].wait_recv()
        multiply(3, i, diag)

    for i in range(CHUNKS):
        own[i].wait()
        multiply(0, i, l, first=i == 0)
    for i in range(CHUNKS):
        to_part[i].wait_recv()
        multiply(1, i, part)

    done = 0
    for i in range(CHUNKS):
        upto = min(n - 1, ((i + 1) * 5 * (n - 1)) // (7 * CHUNKS))
        while done < upto:
            ring_arrive(done)
            done += 1
        arrive(i)

    gate = acc_g[...]
    hid[0] = (gate / (1.0 + jnp.exp(-gate)) * acc_u[...]).astype(BF16)
    h_across = remote(hid.at[0], hid.at[2], h_send.at[0], h_recv.at[0], s, across)
    h_part = remote(hid.at[0], hid.at[1], h_send.at[1], h_recv.at[1], s, part)
    h_pass = remote(hid.at[2], hid.at[3], h_send.at[2], h_recv.at[2], s, part)
    h_across.start()
    h_part.start()
    while done < n - 1:
        ring_arrive(done)
        done += 1
    loads[3].wait()
    loads[4].wait()
    loads[2].wait()
    h_across.wait_recv()
    h_pass.start()

    a = dot(grad[...], ob[...].reshape(tile, tile))
    high, low = split(a)
    a_hi[...] = high
    a_lo[...] = low

    h_part.wait_recv()
    for swap in swaps:
        swap.wait_recv()
    h_pass.wait_recv()
    units = hid.shape[2]
    rows_dev = ib.shape[1]
    count = units // rows_dev
    pieces = []
    for slot, lane in ((0, l), (1, part), (2, across), (3, diag)):
        block = ib[pl.ds(lane * count, count)].reshape(units, tile)
        i_hi, i_lo = split(block)
        h = hid[slot]
        pieces.append(dot(h, i_hi) + dot(h, i_lo))
    high, low = split((pieces[0] + pieces[1]) + (pieces[2] + pieces[3]))
    b_hi[...] = high
    b_lo[...] = low

    group = max(1, 128 // rows_dev)
    size = group * rows_dev
    blocks = n // group

    def sends(dest):
        return remote(
            r_send.at[dest], r_recv.at[s], r_ssem.at[dest], r_rsem.at[s], dest, l)

    def emit(q):
        columns = pl.ds(pl.multiple_of(q * size, size), size)
        bh, bl = b_hi[:, columns], b_lo[:, columns]
        ah, al = a_hi[...], a_lo[...]
        r = dot_first(bh, ah) + (dot_first(bh, al) + dot_first(bl, ah))
        r_send[pl.ds(q * group, group)] = r.astype(BF16).reshape(group, rows_dev, tile)

    @pl.loop(0, blocks)
    def _(d):
        q = lax.rem(s // group + 1 + d, blocks)
        emit(q)
        for g in range(group):
            dest = q * group + g

            @pl.when(dest != s)
            def _():
                sends(dest).start()

    def masks(src):
        member = (2 * order[src]) // n
        second = member.astype(F32)
        return 1.0 - second, second

    first, second = masks(s)
    mine = r_send[s].astype(F32)
    sum0[...] = mine * first
    sum1[...] = mine * second

    @pl.loop(1, n)
    def _(d):
        src = lax.rem(s + n - d, n)
        remote(
            r_send.at[src], r_recv.at[src], r_ssem.at[src], r_rsem.at[src], src, l
        ).wait_recv()
        first, second = masks(src)
        value = r_recv[src].astype(F32)
        sum0[...] += value * first
        sum1[...] += value * second

    r0, r1 = sum0[...], sum1[...]
    out[0] = (r0 * r0 + r1 * r1) * 0.5

    @pl.loop(1, n)
    def _(d):
        sends(lax.rem(s + d, n)).wait_send()

    for copy in to_across + to_part + passed + [h_across, h_part, h_pass] + swaps:
        copy.wait_send()
    for made in steps:
        for copy in made:
            copy.wait_send()


def on_device(
    tokens_in, gate_weight, up_weight, output_grad, input_basis, output_basis, shard_order
):
    n = lax.axis_size("seq")
    tokens, depth = tokens_in.shape
    units = gate_weight.shape[1]
    rows, tile = input_basis.shape
    sem = pltpu.SemaphoreType.DMA
    any_spec = pl.BlockSpec(memory_space=pl.ANY)
    return pl.pallas_call(
        functools.partial(kernel, n),
        out_shape=jax.ShapeDtypeStruct((1, rows, tile), F32),
        in_specs=[pl.BlockSpec(memory_space=pltpu.SMEM)] + [any_spec] * 6,
        out_specs=pl.BlockSpec(memory_space=pltpu.VMEM),
        scratch_shapes=[
            pltpu.VMEM(gate_weight.shape, BF16),
            pltpu.VMEM(up_weight.shape, BF16),
            pltpu.VMEM((4, CHUNKS, tokens, depth // CHUNKS), BF16),
            pltpu.VMEM((tokens, tile), BF16),
            pltpu.VMEM((n, rows, tile), F32),
            pltpu.VMEM((n, rows, tile), BF16),
            pltpu.VMEM((tokens, units), F32),
            pltpu.VMEM((tokens, units), F32),
            pltpu.VMEM((4, tokens, units), BF16),
            pltpu.VMEM((tokens, tile), BF16),
            pltpu.VMEM((tokens, tile), BF16),
            pltpu.VMEM((tokens, tile), BF16),
            pltpu.VMEM((tokens, tile), BF16),
            pltpu.VMEM((n, rows, tile), BF16),
            pltpu.VMEM((n, rows, tile), BF16),
            pltpu.VMEM((rows, tile), F32),
            pltpu.VMEM((rows, tile), F32),
            sem((5,)), sem((CHUNKS,)),
            sem((CHUNKS,)), sem((CHUNKS,)), sem((CHUNKS,)), sem((CHUNKS,)),
            sem((CHUNKS,)), sem((CHUNKS,)),
            sem((3,)), sem((3,)),
            sem((2, n - 1)), sem((2, n - 1)), sem((2, n - 1)), sem((2, n - 1)),
            sem((2, n - 1)), sem((2, n - 1)),
            sem((n,)), sem((n,)),
        ],
        compiler_params=pltpu.CompilerParams(
            collective_id=0, has_side_effects=True, vmem_limit_bytes=60 * 2**20
        ),
    )(
        shard_order, tokens_in, gate_weight, up_weight, output_grad,
        input_basis, output_basis[0].astype(BF16),
    )


def solution(mesh):
    return jax.shard_map(
        on_device,
        mesh=mesh,
        in_specs=(
            P("seq", "lane"),
            P(None, "lane"),
            P(None, "lane"),
            P("seq", "lane"),
            P("seq", None),
            P("lane", "seq", None),
            P(),
        ),
        out_specs=P("lane", "seq", None),
        check_vma=False,
    )
```

time: 420 us -> 115 us (0.27); the launches traced: 415 us -> 115 us
  waiting for transfers between devices: 347 us -> 0 us
  Pallas kernels: 0 us -> 111 us
  matrix products: 29.7 us -> 0 us
  between operations: 13.9 us -> 0.01 us
  starting transfers between devices: 10.6 us -> 0 us
  other arithmetic: 7.96 us -> 1.78 us
  local copies, waits for them, and re-layouts: 6.37 us -> 1.89 us
    all_gather x4 -> x0, waiting for transfers between devices: 152 us -> none  [the longest x1 79.5 us: on_device(): lax.all_gather(output_basis[0], 'seq', axis=0, tiled=True)]
    reduce_scatter x1 -> x0, waiting for transfers between devices: 146 us -> none  [on_device(): slab = lax.psum_scatter(stacked, 'seq', scatter_dimension=1, tiled=True)]
    pallas_call x0 -> x1, Pallas kernels: none -> 111 us  [on_device(): pl.pallas_call(functools.partial(kernel, n), out_shape=jax.ShapeDtypeStru...]
    all_to_all x2 -> x0, waiting for transfers between devices: 46 us -> none  [the longest x1 46 us: on_device(): lax.all_to_all(partial_value, 'lane', split_axis=0, concat_axis=2, tiled=...]
    dot_general x4 -> x0, matrix products: 29.7 us -> none  [the longest x1 12.2 us: on_device(): lax.dot_general(full_grads, hidden, (((0,), (0,)), ((), ())), preferred_e...]
    all_to_all x2 -> x0, starting transfers between devices: 10.5 us -> none  [the longest x1 5.29 us: on_device(): lax.all_to_all(partial_value, 'lane', split_axis=0, concat_axis=2, tiled=...]
    reshape x1 -> x0, local copies, waits for them, and re-layouts: 4.74 us -> none  [on_device(): partial_value = partial_value.reshape(lane_count, tile, columns)]
  transfers between devices with their start and end apart: 7 -> 0, of which waited for: 5 -> 0; matrix products, arithmetic and copies ran while one was open for 9% -> 0% of each run, Pallas kernels for 0% -> 0%
where the time goes in v1:
time: 115 us
  Pallas kernels  111 us (97%)
  local copies, waits for them, and re-layouts  1.89 us (2%)
  other arithmetic  1.78 us (2%)
    pallas_call x1, Pallas kernels, on_device(): pl.pallas_call(functools.partial(kernel, n), out_shape=jax.ShapeDtypeStru...  111 us

profile of v1, /device:TPU:13, one launch (start us, length us, event | category | flops | bytes accessed | tf_op | source)
XLA Modules:
  0.0 114.8 jit_solution(10271936855487143094)
XLA Ops:
  0.0 1.8 %convert_bitcast_fusion.ob_in = bf16[128,1024]{1,0:T(8,128)(2,1)} fusion(f32[1,128,1024]{2,1,0:T(8,128)} %param.12), kind=kLoop, calls=%fused_computation | loop fusion | flops 131072 | bytes 786432 | tf_op jit(solution)/shard_map/convert_element_type | solution.py:320
  1.8 111.1 %shard_map.73 = f32[1,128,1024]{2,1,0:T(8,128)} custom-call(s32[8]{0:T(128)} %order.1, bf16[384,2048]{1,0:T(8,128)(2,1)} %tok_in.1, bf16[8192,256]{1,0:T(8,128)(2,1)} %gate_in.1, bf16[8192,256]{1,0:T(8,128)(2,1)} %up_in.1, bf16[384,1024]{1,0:T(8,128)(2,1)} %grad_in.1, f32[128,1024]{1,0:T(8,128)} %ib_in.1, bf16[128,1024]{1,0:T(8,128)(2,1)} %convert_bitcast_fusion.ob_in), custom_call_target="tpu_custom_call" | custom-call | tf_op jit(solution)/shard_map/pallas_call | solution.py:284
  112.9 1.9 %copy.9 = f32[1,128,1024]{2,1,0:T(8,128)} copy(f32[1,128,1024]{2,1,0:T(8,128)} %shard_map.73) | data formatting | bytes 1048576

commit v2 on v1

--- a/solution.py
+++ b/solution.py
@@ -118,11 +118,10 @@
     swaps = []
 
     def ring_arrive(t):
-        for copy in steps[t]:
+        for j, copy in enumerate(steps[t]):
             copy.wait_recv()
-        if t + 1 < n - 1:
-            for copy in steps[t + 1]:
-                copy.start()
+            if t + 1 < n - 1:
+                steps[t + 1][j].start()
         for way in range(2):
             owner = seq_of(ring - t - 1) if way == 0 else seq_of(ring + t + 1)
             small = pl.ds(pl.multiple_of(ib_base + way * narrow, narrow), narrow)
@@ -167,7 +166,7 @@
 
     done = 0
     for i in range(CHUNKS):
-        upto = min(n - 1, ((i + 1) * 5 * (n - 1)) // (7 * CHUNKS))
+        upto = 5 * (n - 1) // 7
         while done < upto:
             ring_arrive(done)
             done += 1
@@ -186,13 +185,12 @@
     loads[3].wait()
     loads[4].wait()
     loads[2].wait()
-    h_across.wait_recv()
-    h_pass.start()
-
     a = dot(grad[...], ob[...].reshape(tile, tile))
     high, low = split(a)
     a_hi[...] = high
     a_lo[...] = low
+    h_across.wait_recv()
+    h_pass.start()
 
     h_part.wait_recv()
     for swap in swaps:

time: 115 us -> 108 us (0.939)
  Pallas kernels: 111 us -> 104 us
    pallas_call x1, Pallas kernels: 111 us -> 104 us  [on_device(): pl.pallas_call(functools.partial(kernel, n), out_shape=jax.ShapeDtypeStru...]
where the time goes in v2:
time: 108 us
  Pallas kernels  104 us (96%)
  local copies, waits for them, and re-layouts  1.89 us (2%)
  other arithmetic  1.78 us (2%)
    pallas_call x1, Pallas kernels, on_device(): pl.pallas_call(functools.partial(kernel, n), out_shape=jax.ShapeDtypeStru...  104 us

profile of v2, /device:TPU:13, one launch (start us, length us, event | category | flops | bytes accessed | tf_op | source)
XLA Modules:
  0.0 107.8 jit_solution(878304956225085827)
XLA Ops:
  0.0 1.8 %convert_bitcast_fusion.ob_in = bf16[128,1024]{1,0:T(8,128)(2,1)} fusion(f32[1,128,1024]{2,1,0:T(8,128)} %param.12), kind=kLoop, calls=%fused_computation | loop fusion | flops 131072 | bytes 786432 | tf_op jit(solution)/shard_map/convert_element_type | solution.py:318
  1.8 104.1 %shard_map.73 = f32[1,128,1024]{2,1,0:T(8,128)} custom-call(s32[8]{0:T(128)} %order.1, bf16[384,2048]{1,0:T(8,128)(2,1)} %tok_in.1, bf16[8192,256]{1,0:T(8,128)(2,1)} %gate_in.1, bf16[8192,256]{1,0:T(8,128)(2,1)} %up_in.1, bf16[384,1024]{1,0:T(8,128)(2,1)} %grad_in.1, f32[128,1024]{1,0:T(8,128)} %ib_in.1, bf16[128,1024]{1,0:T(8,128)(2,1)} %convert_bitcast_fusion.ob_in), custom_call_target="tpu_custom_call" | custom-call | tf_op jit(solution)/shard_map/pallas_call | solution.py:282
  105.9 1.9 %copy.9 = f32[1,128,1024]{2,1,0:T(8,128)} copy(f32[1,128,1024]{2,1,0:T(8,128)} %shard_map.73) | data formatting | bytes 1048576
